TPU v7x, 32 devices: a whole 2x2x4 slice. The times are simulated.
32 devices in a mesh: row: 8 (over y, x, core), col: 4 (over z).
Axes of the slice: x: 2, y: 2, z: 4, core: 2. Of those that a mesh axis runs over, the one named last changes fastest.
Arguments:
- inverse_blocks: float32 [4096, 4096], P('row', 'col'), may hold values from -0.09375 to 0.09375
- panel: bfloat16 [4096, 4096], P('row', 'col'), may hold values from -1.5 to 1.5
- diag_inverse: float32 [512, 4096], P('row', 'col'), may hold values from -6 to 6
- members: int32 [8, 8], replicated, may hold values from 0 to 7, each once within a row
- counts: int32 [8], replicated, may hold values from 1 to 8, as said below
Outputs:
- offdiag: float32 [4096, 4096], P('row', 'col')
- new_diag: float32 [512, 4096], P('row', 'col')
Inputs may be any that keep to these rules, and one draw needn't show every extreme that they name: Each row of members names every ancestor once. `counts`: some supernode lists all 8 ancestors and some lists one.
All inputs are finite; a program needn't handle non-finite values.
Results may differ from a plain program's by a relative error of at most 0.0003.
Values may be sent and summed in bfloat16 or wider, within the bound.
A program may use at most 128 MiB of HBM per device.

v0:
```python
import jax
import jax.numpy as jnp
from jax import lax
from jax.sharding import PartitionSpec as P

B = 512


def body(inverse_blocks, panel, diag_inverse, members, counts):
    rows_dev = panel.shape[0]
    sup_count = panel.shape[1] // B
    row_index = lax.axis_index("row")
    col_index = lax.axis_index("col")
    ancestor = row_index * rows_dev // B
    first_sup = col_index * sup_count
    local_members = lax.dynamic_slice_in_dim(members, first_sup, sup_count, 0)
    local_counts = lax.dynamic_slice_in_dim(counts, first_sup, sup_count, 0)
    slot_index = jnp.arange(members.shape[1], dtype=jnp.int32)
    live_slot = slot_index[None, :] < local_counts[:, None]
    row_mask = jnp.sum(
        jnp.where((local_members == ancestor) & live_slot, 1.0, 0.0).astype(jnp.float32), axis=1
    )
    column_mask = jnp.repeat(row_mask, B)
    masked = panel * column_mask.astype(jnp.bfloat16)[None, :]
    inverse_rows = lax.all_gather(inverse_blocks, "col", axis=1, tiled=True)
    running = jnp.dot(
        inverse_rows,
        lax.all_gather(masked, "row", axis=0, tiled=True).astype(jnp.float32),
        precision=lax.Precision.HIGHEST,
    )
    offdiag = -(running * column_mask[None, :])
    masked_wide = masked.astype(jnp.float32).reshape(rows_dev, sup_count, B)
    offdiag_wide = offdiag.reshape(rows_dev, sup_count, B)
    diag_terms = jnp.einsum(
        "ikc,ikd->ckd", masked_wide, offdiag_wide, precision=lax.Precision.HIGHEST
    )
    summed = lax.psum_scatter(
        diag_terms.reshape(B, sup_count * B), "row", scatter_dimension=0, tiled=True
    )
    return (offdiag, diag_inverse - summed)


def solution(mesh):
    return jax.shard_map(
        body,
        mesh=mesh,
        in_specs=(P("row", "col"), P("row", "col"), P("row", "col"), P(), P()),
        out_specs=(P("row", "col"), P("row", "col")),
        check_vma=False,
    )
```

profile of v0, /device:TPU:0, one launch (start us, length us, event | category | flops | bytes accessed | tf_op | source)
XLA Modules:
  0.0 291.6 jit_solution(4853133798508175931)
XLA Ops:
  7.2 0.0 copy-start.3
  7.2 0.0 copy-start.1
  7.2 0.0 all-gather.5.cloned.1.call-start
  7.2 0.7 all-gather.5.cloned.1.call-update
  7.9 0.0 all-gather.3.cloned.1.call-start
  8.0 0.0 copy-done.3
  8.0 0.1 dynamic_slice.7
  8.1 0.9 fusion.3
  8.9 0.1 broadcast_bitcast_fusion
  9.0 1.0 broadcast_multiply_fusion
  10.1 0.0 all-gather.3.cloned.1.call-update
  10.1 0.0 copy-start
  10.1 0.0 reduce-scatter.2.cloned.1.call-start
  10.2 151.8 %all-gather.5.cloned.1.call-done = f32[512,4096]{1,0:T(8,128)} async-done(((f32[512,1024]{1,0:T(8,128)}), f32[512,4096]{1,0:T(8,128)}) %all-gather.5.cloned.1.call-update) | async-done | bytes 8388624 | tf_op jit(solution)/shard_map/all_gather | solution.py:25
  162.0 55.1 %all-gather.3.cloned.1.call-done = bf16[4096,1024]{1,0:T(8,128)(2,1)} async-done(((bf16[512,1024]{1,0:T(8,128)(2,1)}), bf16[4096,1024]{1,0:T(8,128)(2,1)}) %all-gather.3.cloned.1.call-update) | async-done | bytes 8388624 | tf_op jit(solution)/shard_map/all_gather | solution.py:28
  217.0 18.9 %multiply_negate_fusion = f32[1024,512]{1,0:T(8,128)S(1)} fusion(bf16[4096,1024]{1,0:T(8,128)(2,1)} %all-gather.3.cloned.1.call-done, f32[512,4096]{1,0:T(8,128)} %all-gather.5.cloned.1.call-done, f32[1024]{0:T(1024)S(1)} %bitcast.21), kind=kOutput, calls=%fused_computation | convolution fusion | flops 25770852352 | bytes 18878464 | tf_op jit(solution)/shard_map/dot_general | solution.py:26
  235.9 0.0 copy-done
  235.9 3.1 %fusion = f32[2,512,512]{2,1,0:T(8,128)} fusion(f32[512,2,512]{0,2,1:T(8,128)S(1)} %bitcast.17, bf16[64,2,8,512]{3,2,1,0:T(8,128)(2,1)S(1)} %bitcast.16), kind=kOutput, calls=%fused_computation.1 | convolution fusion | flops 3221225472 | bytes 5242880 | tf_op jit(solution)/shard_map/ikc,ikd->ckd/dot_general | solution.py:34
  239.0 2.9 %copy.8 = f32[512,1024]{1,0:T(8,128)} copy(f32[512,1024]{0,1:T(8,128)} %bitcast.19) | data formatting | bytes 4194304 | tf_op jit(solution)/shard_map/reshape | solution.py:38
  242.0 0.0 reduce-scatter.2.cloned.1.call-update
  242.0 0.0 copy-start.2
  242.0 1.8 copy.9
  243.8 39.6 %reduce-scatter.2.cloned.1.call-done = f32[64,1024]{1,0:T(8,128)} async-done(((f32[512,1024]{1,0:T(8,128)}), f32[64,1024]{1,0:T(8,128)}) %reduce-scatter.2.cloned.1.call-update) | async-done | bytes 262160 | tf_op jit(solution)/shard_map/reduce_scatter | solution.py:37
  283.4 1.7 sub.8
  (4 shorter events, 0.0 us)
Async XLA Ops:
  7.2 0.8 copy-start.3
  7.2 1.9 copy-start.1
  7.2 154.8 %all-gather.5.cloned.1.call-start = ((), (), s32[]{:S(2)}) async-start(), calls=%async_computation.2 | async-start | bytes 10485760 | tf_op jit(solution)/shard_map/all_gather | solution.py:25
  7.9 209.1 %all-gather.3.cloned.1.call-start = ((), (), s32[]{:S(2)}) async-start(), calls=%async_computation.1 | async-start | bytes 9437184 | tf_op jit(solution)/shard_map/all_gather | solution.py:28
  10.1 225.8 %copy-start = (bf16[512,1024]{1,0:T(8,128)(2,1)S(1)}, bf16[512,1024]{1,0:T(8,128)(2,1)}, u32[]{:S(2)}) copy-start(bf16[512,1024]{1,0:T(8,128)(2,1)} %broadcast_multiply_fusion) | copy-start | bytes 3145732
  10.1 273.3 %reduce-scatter.2.cloned.1.call-start = ((), (), s32[]{:S(2)}) async-start(), calls=%async_computation.3 | async-start | bytes 2359296 | tf_op jit(solution)/shard_map/reduce_scatter | solution.py:37
  242.0 41.4 %copy-start.2 = (f32[64,1024]{1,0:T(8,128)S(1)}, f32[64,1024]{1,0:T(8,128)}, u32[]{:S(2)}) copy-start(f32[64,1024]{1,0:T(8,128)} %param.7) | copy-start | bytes 786436
Sparse Core Ops, SparseCore 0:
  9.6 152.3 all-gather.4
  164.4 52.5 all-gather.2
  242.1 41.2 reduce-scatter.1
where the time goes:
time: 292 us
  waiting for transfers between devices  247 us (85%)
  matrix products  22 us (8%)
  between operations  13.8 us (5%)
  local copies, waits for them, and re-layouts  4.93 us (2%)
  other arithmetic  3.6 us (1%)
    all_gather x1, waiting for transfers between devices, body(): inverse_rows = lax.all_gather(inverse_blocks, 'col', axis=1, tiled=True)  152 us
    all_gather x1, waiting for transfers between devices, body(): lax.all_gather(masked, 'row', axis=0, tiled=True).astype(jnp.float32)  55.1 us
    reduce_scatter x1, waiting for transfers between devices, body(): lax.psum_scatter(diag_terms.reshape(B, sup_count * B), 'row', scatter_dim...  39.6 us
    dot_general x1, matrix products, body(): jnp.dot(inverse_rows, lax.all_gather(masked, 'row', axis=0, tiled=True).a...  18.9 us
  transfers between devices with their start and end apart: 3, of which 3 were waited for; matrix products, arithmetic and copies ran while one was open for 1% of the time, Pallas kernels for 0%

commit v1 on v0

v1 whole, which is shorter than its diff:
```python
import jax
import jax.numpy as jnp
from jax import lax
from jax.sharding import PartitionSpec as P

B = 512


def quantize(block):
    peak = jnp.max(jnp.abs(block), axis=1, keepdims=True)
    live = peak > 1e-30
    safe = jnp.where(live, peak, 1.0)
    coded = jnp.round(block * (32767.0 / safe)).astype(jnp.int16)
    return jnp.where(live, coded, 0), safe * (1.0 / 32767.0)


def split_code(coded):
    wide = coded.astype(jnp.int32)
    high = (wide + 64) & -128
    return high.astype(jnp.bfloat16), (wide - high).astype(jnp.bfloat16)


def column_masks(members, counts, ancestor, first_sup, sup_count):
    local_members = lax.dynamic_slice_in_dim(members, first_sup, sup_count, 0)
    local_counts = lax.dynamic_slice_in_dim(counts, first_sup, sup_count, 0)
    slot_index = jnp.arange(members.shape[1], dtype=jnp.int32)
    live_slot = slot_index[None, :] < local_counts[:, None]
    row_mask = jnp.sum(
        jnp.where((local_members == ancestor) & live_slot, 1.0, 0.0).astype(jnp.float32), axis=1
    )
    return jnp.repeat(row_mask, B)


def body(inverse_blocks, panel, diag_inverse, members, counts):
    rows_dev, cols_dev = panel.shape
    sup_count = cols_dev // B
    depth = inverse_blocks.shape[1]
    ancestor = lax.axis_index("row") * rows_dev // B
    column_mask = column_masks(members, counts, ancestor, lax.axis_index("col") * sup_count, sup_count)
    masked = panel * column_mask.astype(jnp.bfloat16)[None, :]
    coded, scale = quantize(inverse_blocks)
    coded_all = lax.all_gather(coded, "col", axis=0, tiled=False)
    scale_all = lax.all_gather(scale, "col", axis=0, tiled=False)
    masked_all = lax.all_gather(masked, "row", axis=0, tiled=True)
    running = jnp.zeros((rows_dev, cols_dev), jnp.float32)
    for shard in range(coded_all.shape[0]):
        high, low = split_code(coded_all[shard])
        part = masked_all[shard * depth : (shard + 1) * depth]
        term = jnp.dot(high, part, preferred_element_type=jnp.float32) + jnp.dot(
            low, part, preferred_element_type=jnp.float32
        )
        running = running + scale_all[shard] * term
    offdiag = -(running * column_mask[None, :])
    off_high = lax.reduce_precision(offdiag, 8, 7)
    off_low = (offdiag - off_high).astype(jnp.bfloat16).reshape(rows_dev, sup_count, B)
    off_high = off_high.astype(jnp.bfloat16).reshape(rows_dev, sup_count, B)
    masked_blocks = masked.reshape(rows_dev, sup_count, B)
    diag_terms = jnp.einsum(
        "ikc,ikd->ckd", masked_blocks, off_high, preferred_element_type=jnp.float32
    ) + jnp.einsum("ikc,ikd->ckd", masked_blocks, off_low, preferred_element_type=jnp.float32)
    summed = lax.psum_scatter(
        diag_terms.reshape(B, sup_count * B), "row", scatter_dimension=0, tiled=True
    )
    return (offdiag, diag_inverse - summed)


def solution(mesh):
    return jax.shard_map(
        body,
        mesh=mesh,
        in_specs=(P("row", "col"), P("row", "col"), P("row", "col"), P(), P()),
        out_specs=(P("row", "col"), P("row", "col")),
        check_vma=False,
    )
```

time: 292 us -> 168 us (0.58)
  waiting for transfers between devices: 247 us -> 43.1 us
  blocking collectives: 0 us -> 82.2 us
  matrix products: 22 us -> 17.7 us
    all_gather x2 -> x1, waiting for transfers between devices: 207 us -> 0.01 us  [body(): masked_all = lax.all_gather(masked, 'row', axis=0, tiled=True)]
    all_gather x0 -> x2, blocking collectives: none -> 82.2 us  [the longest x1 68.6 us: body(): coded_all = lax.all_gather(coded, 'col', axis=0, tiled=False)]
    dot_general x2 -> x10, matrix products: 22 us -> 17.7 us  [the longest x4 11.2 us: body(): jnp.dot(high, part, preferred_element_type=jnp.float32)]
    reduce_scatter x1, waiting for transfers between devices: 39.6 us -> 43.1 us  [body(): lax.psum_scatter(diag_terms.reshape(B, sup_count * B), 'row', scatter_dim...]
  transfers between devices with their start and end apart: 3 -> 2, of which waited for: 3 -> 1; matrix products, arithmetic and copies ran while one was open for 1% -> 0% of each run, Pallas kernels for 0% -> 0%
where the time goes in v1:
time: 168 us
  blocking collectives  82.2 us (49%)
  waiting for transfers between devices  43.1 us (26%)
  matrix products  17.7 us (11%)
  between operations  14.2 us (8%)
  other arithmetic  5.59 us (3%)
  local copies, waits for them, and re-layouts  5.3 us (3%)
    all_gather x1, blocking collectives, body(): coded_all = lax.all_gather(coded, 'col', axis=0, tiled=False)  68.6 us
    reduce_scatter x1, waiting for transfers between devices, body(): lax.psum_scatter(diag_terms.reshape(B, sup_count * B), 'row', scatter_dim...  43.1 us
    all_gather x1, blocking collectives, body(): scale_all = lax.all_gather(scale, 'col', axis=0, tiled=False)  13.5 us
    dot_general x4, matrix products, body(): jnp.dot(high, part, preferred_element_type=jnp.float32)  11.2 us
    dot_general x4, matrix products, body(): jnp.dot(low, part, preferred_element_type=jnp.float32)  5.06 us
  transfers between devices with their start and end apart: 2, of which 1 were waited for; matrix products, arithmetic and copies ran while one was open for 0% of the time, Pallas kernels for 0%

profile of v1, /device:TPU:0, one launch (start us, length us, event | category | flops | bytes accessed | tf_op | source)
XLA Modules:
  0.0 168.2 jit_solution(2988183618766830160)
XLA Ops:
  7.2 0.9 dynamic_slice.7
  8.1 0.9 fusion.70
  9.1 2.3 %broadcast_multiply_fusion = bf16[512,1024]{1,0:T(8,128)(2,1)} fusion(bf16[512,1024]{1,0:T(8,128)(2,1)} %param.6, bf16[1024]{0:T(1024)(128)(2,1)S(1)} %convert_element_type.70), kind=kLoop, calls=%fused_computation.73 | loop fusion | flops 524288 | bytes 2099200 | tf_op jit(solution)/shard_map/mul | solution.py:40
  11.5 0.2 abs_reduce_fusion
  11.7 13.5 %all_gather.13 = f32[4,512,1]{1,2,0:T(1,128)S(1)} all-gather(f32[1,512,1]{1,2,0:T(1,128)S(1)} %fusion.69), channel_id=1, replica_groups=mesh['row'=8,'col'=4] {'col'}, dimensions={0}, use_global_device_ids=true | all-gather | bytes 10240 | tf_op jit(solution)/shard_map/all_gather | solution.py:43
  25.3 0.5 fusion.31
  25.7 68.6 %all-gather.5 = s16[2048,1024]{1,0:T(8,128)(2,1)} all-gather(s16[512,1024]{1,0:T(8,128)(2,1)S(1)} %fusion.31), channel_id=2, replica_groups=mesh['row'=8,'col'=4] {'col'}, dimensions={0}, use_global_device_ids=true | all-gather | bytes 5242880 | tf_op jit(solution)/shard_map/all_gather | solution.py:42
  94.4 3.3 %fusion.23 = f32[512,1024]{1,0:T(8,128)S(1)} fusion(bf16[4096,1024]{1,0:T(8,128)(2,1)} %all-gather.4.cloned.1.call-done, s16[2048,1024]{1,0:T(8,128)(2,1)} %all-gather.5), kind=kOutput, calls=%fused_computation.36 | convolution fusion | flops 1075838976 | bytes 5242880 | tf_op jit(solution)/shard_map/dot_general | solution.py:49
  97.7 3.0 %fusion.19 = f32[512,1024]{1,0:T(8,128)S(1)} fusion(bf16[4096,1024]{1,0:T(8,128)(2,1)} %all-gather.4.cloned.1.call-done, s16[2048,1024]{1,0:T(8,128)(2,1)S(1)} %copy-done.2), kind=kOutput, calls=%fused_computation.32 | convolution fusion | flops 1075838976 | bytes 5242880 | tf_op jit(solution)/shard_map/dot_general | solution.py:49
  100.8 0.1 slice-done.1
  100.9 1.3 fusion.15
  102.1 1.3 fusion.17
  103.4 1.3 fusion.21
  104.7 1.3 fusion.25
  105.9 1.3 fusion.13
  107.2 3.6 %fusion.12 = (bf16[512,1024]{1,0:T(8,128)(2,1)S(1)}, bf16[512,1024]{1,0:T(8,128)(2,1)S(1)}, f32[512,1024]{1,0:T(8,128)}) fusion(f32[1024]{0:T(1024)S(1)} %bitcast.29, f32[512,1024]{1,0:T(8,128)S(1)} %fusion.15, f32[512,1024]{1,0:T(8,128)S(1)} %fusion.13, f32[512]{0:T(512)S(1)} %bitcast.32, f32[512,1024]{1,0:T(8,128)S(1)} %fusion.19, ...), kind=kOutput, calls=%fused_computation.22 | convolution fusion | flops 1084751872 | bytes 22032384 | tf_op jit(solution)/shard_map/dot_general | solution.py:49
  110.8 1.3 copy.23
  112.2 0.5 copy.22
  112.7 0.7 fusion.41
  113.4 0.5 copy-done.3
  113.9 0.7 convolution_add_fusion
  114.7 1.9 %copy.21 = f32[512,1024]{1,0:T(8,128)} copy(f32[512,1024]{0,1:T(8,128)S(1)} %bitcast.23) | data formatting | bytes 4194304 | tf_op jit(solution)/shard_map/reshape | solution.py:62
  116.6 43.1 %reduce-scatter.2.cloned.1.call-done = f32[64,1024]{1,0:T(8,128)} async-done(((f32[512,1024]{1,0:T(8,128)}), f32[64,1024]{1,0:T(8,128)}) %reduce-scatter.2.cloned.1.call-update) | async-done | bytes 262160 | tf_op jit(solution)/shard_map/reduce_scatter | solution.py:61
  159.7 1.7 sub.28
  (25 shorter events, 0.2 us)
Async XLA Ops:
  7.2 4.3 %copy-start.1 = (f32[512,1024]{1,0:T(8,128)S(1)}, f32[512,1024]{1,0:T(8,128)}, u32[]{:S(2)}) copy-start(f32[512,1024]{1,0:T(8,128)} %param.5) | copy-start | bytes 6291460
  7.2 87.2 %all-gather.4.cloned.1.call-start = ((), (), s32[]{:S(2)}) async-start(), calls=%async_computation.1 | async-start | bytes 9437184 | tf_op jit(solution)/shard_map/all_gather | solution.py:44
  11.4 148.3 %reduce-scatter.2.cloned.1.call-start = ((), (), s32[]{:S(2)}) async-start(), calls=%async_computation.2 | async-start | bytes 2359296 | tf_op jit(solution)/shard_map/reduce_scatter | solution.py:61
  94.4 3.3 %copy-start.2 = (s16[2048,1024]{1,0:T(8,128)(2,1)S(1)}, s16[2048,1024]{1,0:T(8,128)(2,1)}, u32[]{:S(2)}) copy-start(s16[2048,1024]{1,0:T(8,128)(2,1)} %all-gather.5) | copy-start | bytes 12582916
  94.4 6.4 %slice-start = ((s8[8388608]{0:T(1024)(128)(4,1)}), s8[4194304]{0:T(1024)(128)(4,1)S(1)}, s32[]{:S(2)}) async-start(s8[8388608]{0:T(1024)(128)(4,1)} %bitcast.26), calls=%async_computation.3 | async-start | bytes 8388608
  97.7 3.1 %slice-start.1 = ((s8[8388608]{0:T(1024)(128)(4,1)}), s8[4194304]{0:T(1024)(128)(4,1)S(1)}, s32[]{:S(2)}) async-start(s8[8388608]{0:T(1024)(128)(4,1)} %bitcast.26), calls=%async_computation.4 | async-start | bytes 8388608
  110.8 1.9 %copy-start = (bf16[512,1024]{1,0:T(8,128)(2,1)S(1)}, bf16[512,1024]{1,0:T(8,128)(2,1)}, u32[]{:S(2)}) copy-start(bf16[512,1024]{1,0:T(8,128)(2,1)} %broadcast_multiply_fusion) | copy-start | bytes 3145732
  112.7 1.2 copy-start.3
  116.6 43.1 %copy-start.4 = (f32[64,1024]{1,0:T(8,128)S(1)}, f32[64,1024]{1,0:T(8,128)}, u32[]{:S(2)}) copy-start(f32[64,1024]{1,0:T(8,128)} %param.7) | copy-start | bytes 786436
Sparse Core Ops, SparseCore 0:
  11.5 57.0 all-gather.3
  116.7 42.9 reduce-scatter.1

commit v2 on v1

--- a/solution.py
+++ b/solution.py
@@ -1,6 +1,8 @@
 import jax
 import jax.numpy as jnp
 from jax import lax
+from jax.experimental import pallas as pl
+from jax.experimental.pallas import tpu as pltpu
 from jax.sharding import PartitionSpec as P
 
 B = 512
@@ -29,6 +31,312 @@
         jnp.where((local_members == ancestor) & live_slot, 1.0, 0.0).astype(jnp.float32), axis=1
     )
     return jnp.repeat(row_mask, B)
+
+
+MESH = pl.DeviceIdType.MESH
+PIECE = 128
+TILE = 256
+
+
+def fused_kernel(
+    inv_ref, panel_ref, mask_ref, diag_ref, off_ref, new_ref,
+    coded, scales, wide_scale, blocks, stacked, partial, from_twin, chip_sum, from_chips,
+    a_recv, a_right, a_left, s_recv, s_right, s_left,
+    p_recv, p_send, p_twin, t_recv, t_send, c_recv, c_send,
+):
+    n = coded.shape[0]
+    rows, depth = inv_ref.shape
+    cols = panel_ref.shape[1]
+    pieces = rows // PIECE
+    me = lax.axis_index("row")
+    z = lax.axis_index("col")
+    chip, core = lax.div(me, 2), lax.rem(me, 2)
+    y, x = lax.div(chip, 2), lax.rem(chip, 2)
+    twin = chip * 2 + (1 - core)
+    others = (y * 2 + (1 - x), (1 - y) * 2 + x, (1 - y) * 2 + (1 - x))
+
+    def far(src, dst, send, recv, row, col):
+        return pltpu.make_async_remote_copy(
+            src_ref=src, dst_ref=dst, send_sem=send, recv_sem=recv,
+            device_id=(row, col), device_id_type=MESH,
+        )
+
+    def right_piece(c, p):
+        ref = coded.at[c, pl.ds(pl.multiple_of(p * PIECE, PIECE), PIECE)]
+        return far(ref, ref, a_right.at[c, p], a_recv.at[c, p], me, z + 1)
+
+    def left_piece(c, p):
+        ref = coded.at[c, pl.ds(pl.multiple_of(p * PIECE, PIECE), PIECE)]
+        return far(ref, ref, a_left.at[c, p], a_recv.at[c, p], me, z - 1)
+
+    def right_scale(c):
+        return far(scales.at[c], scales.at[c], s_right.at[c], s_recv.at[c], me, z + 1)
+
+    def left_scale(c):
+        return far(scales.at[c], scales.at[c], s_left.at[c], s_recv.at[c], me, z - 1)
+
+    def panel_to(d):
+        return far(blocks.at[me], blocks.at[me], p_send.at[d], p_recv.at[me], others[d] * 2 + core, z)
+
+    def panel_twin(d):
+        r = me if d == 3 else others[d] * 2 + core
+        return far(blocks.at[r], blocks.at[r], p_twin.at[d], p_recv.at[r], twin, z)
+
+    def panel_arrived(r):
+        far(blocks.at[r], blocks.at[r], p_twin.at[0], p_recv.at[r], twin, z).wait_recv()
+
+    barrier = pltpu.get_barrier_semaphore()
+    for row in [twin] + [o * 2 + core for o in others]:
+        pl.semaphore_signal(barrier, inc=1, device_id=(row, z), device_id_type=MESH)
+
+    @pl.when(z > 0)
+    def _():
+        pl.semaphore_signal(barrier, inc=1, device_id=(me, z - 1), device_id_type=MESH)
+
+    @pl.when(z < n - 1)
+    def _():
+        pl.semaphore_signal(barrier, inc=1, device_id=(me, z + 1), device_id_type=MESH)
+
+    block = inv_ref[...]
+    peak = jnp.max(jnp.abs(block), axis=1, keepdims=True)
+    live = peak > 1e-33
+    safe = jnp.where(live, peak, 1.0)
+    ratio = jnp.where(live, 32767.0 / safe, 0.0)
+    ready = block * ratio
+    ready = ready + jnp.where(ready >= 0.0, 0.5, -0.5)
+    coded[z] = ready.astype(jnp.int32).astype(jnp.int16)
+    step = jnp.broadcast_to(safe * (1.0 / 32767.0), (rows, 128))
+    scales[z] = step.T[:8]
+    blocks[me] = panel_ref[...] * mask_ref[...].astype(jnp.bfloat16)
+
+    pl.semaphore_wait(barrier, 4 + jnp.where(z > 0, 1, 0) + jnp.where(z < n - 1, 1, 0))
+
+    @pl.when(z < n - 1)
+    def _():
+        right_scale(z).start()
+
+        @pl.loop(0, pieces)
+        def _(p):
+            right_piece(z, p).start()
+
+    @pl.when(z > 0)
+    def _():
+        left_scale(z).start()
+
+        @pl.loop(0, pieces)
+        def _(p):
+            left_piece(z, p).start()
+
+    panel_twin(3).start()
+    for d in range(3):
+        panel_to(d).start()
+    off_ref[...] = jnp.zeros_like(off_ref)
+    partial[...] = jnp.zeros_like(partial)
+
+    def relay(s):
+        @pl.loop(0, pieces)
+        def _(p):
+            @pl.when(z >= s)
+            def _():
+                @pl.when(p == 0)
+                def _():
+                    right_scale(z - s).wait_recv()
+
+                right_piece(z - s, p).wait_recv()
+
+                @pl.when(z < n - 1)
+                def _():
+                    @pl.when(p == 0)
+                    def _():
+                        right_scale(z - s).start()
+
+                    right_piece(z - s, p).start()
+
+            @pl.when(z + s < n)
+            def _():
+                @pl.when(p == 0)
+                def _():
+                    left_scale(z + s).wait_recv()
+
+                left_piece(z + s, p).wait_recv()
+
+                @pl.when(z > 0)
+                def _():
+                    @pl.when(p == 0)
+                    def _():
+                        left_scale(z + s).start()
+
+                    left_piece(z + s, p).start()
+
+    def widen(c):
+        eight = scales[c]
+        wide_scale[...] = jnp.concatenate([eight] * 16, axis=0).T
+
+    def accumulate(c, first, count):
+        span = pl.ds(first, count)
+        code = coded[c, span, :].astype(jnp.int32)
+        high = (code + 64) & -128
+        stacked[0:count] = high.astype(jnp.float32).astype(jnp.bfloat16)
+        stacked[count : 2 * count] = (code - high).astype(jnp.float32).astype(jnp.bfloat16)
+        step = wide_scale[span, :]
+        step = jnp.concatenate([step] * (TILE // 128), axis=1)
+
+        @pl.loop(0, cols // TILE)
+        def _(t):
+            tile = pl.ds(pl.multiple_of(t * TILE, TILE), TILE)
+            part = blocks[pl.ds(2 * c, 2), :, tile].reshape(depth, TILE)
+            term = jnp.dot(stacked[0 : 2 * count], part, preferred_element_type=jnp.float32)
+            off_ref[span, tile] += step * (term[:count] + term[count:])
+
+    relay(1)
+    for d in range(2):
+        panel_arrived(others[d] * 2 + core)
+        panel_twin(d).start()
+    relay(2)
+    panel_arrived(others[2] * 2 + core)
+    panel_twin(2).start()
+    panel_arrived(twin)
+    for d in range(3):
+        panel_arrived(others[d] * 2 + (1 - core))
+
+    @pl.loop(0, n)
+    def _(c):
+        @pl.when((c <= z + 2) & (c >= z - 2))
+        def _():
+            widen(c)
+            accumulate(c, 0, rows)
+
+    end = (z == 0) | (z == n - 1)
+    last = n - 1 - z
+
+    @pl.when(z == n - 1)
+    def _():
+        right_scale(last).wait_recv()
+
+    @pl.when(z == 0)
+    def _():
+        left_scale(last).wait_recv()
+
+    @pl.when(end)
+    def _():
+        widen(last)
+
+    @pl.loop(0, pieces)
+    def _(p):
+        first = pl.multiple_of(p * PIECE, PIECE)
+        span = pl.ds(first, PIECE)
+
+        @pl.when(z == n - 1)
+        def _():
+            right_piece(last, p).wait_recv()
+
+        @pl.when(z == 0)
+        def _():
+            left_piece(last, p).wait_recv()
+
+        @pl.when(end)
+        def _():
+            accumulate(last, first, PIECE)
+
+        off = -(off_ref[span, :] * mask_ref[...])
+        off_ref[span, :] = off
+        high = off.astype(jnp.bfloat16)
+        low = (off - high.astype(jnp.float32)).astype(jnp.bfloat16)
+        own = blocks[me, span, :]
+        for k in range(cols // B):
+            part = slice(k * B, (k + 1) * B)
+            left = jnp.concatenate([own[:, part]] * 2, axis=0)
+            both = jnp.concatenate([high[:, part], low[:, part]], axis=0)
+            term = lax.dot_general(
+                left, both, (((0,), (0,)), ((), ())), preferred_element_type=jnp.float32
+            )
+            partial[:, :, part] += term.reshape(8, B // 8, B)
+
+    def to_twin(c):
+        return far(partial.at[2 * c + (1 - core)], from_twin.at[c], t_send.at[c], t_recv.at[c], twin, z)
+
+    def to_chip(d):
+        return far(
+            chip_sum.at[others[d]], from_chips.at[d], c_send.at[d], c_recv.at[d],
+            others[d] * 2 + core, z,
+        )
+
+    order = (others[2], others[0], others[1], chip)
+    for c in order:
+        to_twin(c).start()
+    for d in (2, 0, 1):
+        c = others[d]
+        to_twin(c).wait_recv()
+        chip_sum[c] = partial[2 * c + core] + from_twin[c]
+        to_chip(d).start()
+    to_twin(chip).wait_recv()
+    total = diag_ref[...] - (partial[me] + from_twin[chip])
+    for d in (0, 1, 2):
+        to_chip(d).wait_recv()
+        total = total - from_chips[d]
+    new_ref[...] = total
+
+    for c in order:
+        to_twin(c).wait_send()
+    for d in range(3):
+        to_chip(d).wait_send()
+        panel_to(d).wait_send()
+    for d in range(4):
+        panel_twin(d).wait_send()
+    for s in range(3):
+        @pl.when((z >= s) & (z < n - 1))
+        def _():
+            right_scale(z - s).wait_send()
+
+            @pl.loop(0, pieces)
+            def _(p):
+                right_piece(z - s, p).wait_send()
+
+        @pl.when((z + s < n) & (z > 0))
+        def _():
+            left_scale(z + s).wait_send()
+
+            @pl.loop(0, pieces)
+            def _(p):
+                left_piece(z + s, p).wait_send()
+
+
+def fused_body(inverse_blocks, panel, diag_inverse, members, counts):
+    rows_dev, cols_dev = panel.shape
+    depth = inverse_blocks.shape[1]
+    sup_count = cols_dev // B
+    shards = lax.axis_size("col")
+    pieces = rows_dev // PIECE
+    mask = column_masks(members, counts, lax.axis_index("row"), lax.axis_index("col") * sup_count, sup_count)
+    share = diag_inverse.shape[0]
+    vmem = pl.BlockSpec(memory_space=pltpu.VMEM)
+    dma = pltpu.SemaphoreType.DMA
+    return pl.pallas_call(
+        fused_kernel,
+        out_shape=(
+            jax.ShapeDtypeStruct((rows_dev, cols_dev), jnp.float32),
+            jax.ShapeDtypeStruct((share, cols_dev), jnp.float32),
+        ),
+        in_specs=[vmem] * 4,
+        out_specs=(vmem, vmem),
+        scratch_shapes=[
+            pltpu.VMEM((shards, rows_dev, depth), jnp.int16),
+            pltpu.VMEM((shards, 8, rows_dev), jnp.float32),
+            pltpu.VMEM((rows_dev, 128), jnp.float32),
+            pltpu.VMEM((8, rows_dev, cols_dev), jnp.bfloat16),
+            pltpu.VMEM((2 * rows_dev, depth), jnp.bfloat16),
+            pltpu.VMEM((8, share, cols_dev), jnp.float32),
+            pltpu.VMEM((4, share, cols_dev), jnp.float32),
+            pltpu.VMEM((4, share, cols_dev), jnp.float32),
+            pltpu.VMEM((3, share, cols_dev), jnp.float32),
+            dma((shards, pieces)), dma((shards, pieces)), dma((shards, pieces)),
+            dma((shards,)), dma((shards,)), dma((shards,)),
+            dma((8,)), dma((3,)), dma((4,)), dma((4,)), dma((4,)), dma((3,)), dma((3,)),
+        ],
+        compiler_params=pltpu.CompilerParams(
+            collective_id=0, has_side_effects=True, vmem_limit_bytes=56 * 1024 * 1024
+        ),
+    )(inverse_blocks, panel, mask[None, :], diag_inverse)
 
 
 def body(inverse_blocks, panel, diag_inverse, members, counts):
@@ -65,8 +373,9 @@
 
 
 def solution(mesh):
+    fits = mesh.shape["row"] == 8 and mesh.shape["col"] == 4
     return jax.shard_map(
-        body,
+        fused_body if fits else body,
         mesh=mesh,
         in_specs=(P("row", "col"), P("row", "col"), P("row", "col"), P(), P()),
         out_specs=(P("row", "col"), P("row", "col")),

time: 168 us -> 101 us (0.60)
  Pallas kernels: 0 us -> 94.4 us
  blocking collectives: 82.2 us -> 0 us
  waiting for transfers between devices: 43.1 us -> 0 us
  matrix products: 17.7 us -> 0 us
  between operations: 14.2 us -> 0.65 us
  other arithmetic: 5.59 us -> 0.87 us
    pallas_call x0 -> x1, Pallas kernels: none -> 94.4 us  [fused_body(): pl.pallas_call(fused_kernel, out_shape=(jax.ShapeDtypeStruct((rows_dev, c...]
    all_gather x2 -> x0, blocking collectives: 82.2 us -> none  [the longest x1 68.6 us: body(): coded_all = lax.all_gather(coded, 'col', axis=0, tiled=False)]
    reduce_scatter x1 -> x0, waiting for transfers between devices: 43.1 us -> none  [body(): lax.psum_scatter(diag_terms.reshape(B, sup_count * B), 'row', scatter_dim...]
    dot_general x10 -> x0, matrix products: 17.7 us -> none  [the longest x4 11.2 us: body(): jnp.dot(high, part, preferred_element_type=jnp.float32)]
    unnamed x16 -> x6, local copies, waits for them, and re-layouts: 0.7 us -> 4.58 us
    reshape x3 -> x0, local copies, waits for them, and re-layouts: 3.73 us -> none  [the longest x1 1.87 us: body(): diag_terms.reshape(B, sup_count * B)]
    mul x2 -> x0, other arithmetic: 2.34 us -> none  [the longest x1 2.33 us: body(): masked = panel * column_mask.astype(jnp.bfloat16)[None, :]]
    sub x1 -> x0, other arithmetic: 1.68 us -> none  [body(): return (offdiag, diag_inverse - summed)]
  transfers between devices with their start and end apart: 2 -> 0, of which waited for: 1 -> 0; matrix products, arithmetic and copies ran while one was open for 0% -> 0% of each run, Pallas kernels for 0% -> 0%
where the time goes in v2:
time: 101 us
  Pallas kernels  94.4 us (93%)
  local copies, waits for them, and re-layouts  5.31 us (5%)
    pallas_call x1, Pallas kernels, fused_body(): pl.pallas_call(fused_kernel, out_shape=(jax.ShapeDtypeStruct((rows_dev, c...  94.4 us
    unnamed x6, local copies, waits for them, and re-layouts  4.58 us

profile of v2, /device:TPU:0, one launch (start us, length us, event | category | flops | bytes accessed | tf_op | source)
XLA Modules:
  0.0 101.2 jit_solution(3953556919190937241)
XLA Ops:
  0.6 0.7 dynamic_slice.7
  1.4 0.9 fusion
  2.2 0.1 broadcast_bitcast_fusion
  2.3 0.6 copy.7
  2.9 94.4 %shard_map.68 = (f32[512,1024]{1,0:T(8,128)}, f32[64,1024]{1,0:T(8,128)}) custom-call(f32[512,1024]{1,0:T(8,128)} %inv_ref.1, bf16[512,1024]{1,0:T(8,128)(2,1)} %panel_ref.1, f32[1,1024]{1,0:T(1,128)} %bitcast.4, f32[64,1024]{1,0:T(8,128)} %diag_ref.1), custom_call_target="tpu_custom_call" | custom-call | tf_op jit(solution)/shard_map/pallas_call | solution.py:314
  97.3 0.0 copy-start
  97.3 3.2 %copy.10 = f32[512,1024]{1,0:T(8,128)} copy(f32[512,1024]{1,0:T(8,128)} %get-tuple-element.4) | data formatting | bytes 4194304
  100.5 0.0 copy-done
  100.5 0.7 copy.11
Async XLA Ops:
  97.3 3.2 %copy-start = (f32[64,1024]{1,0:T(8,128)S(1)}, f32[64,1024]{1,0:T(8,128)}, u32[]{:S(2)}) copy-start(f32[64,1024]{1,0:T(8,128)} %get-tuple-element.5) | copy-start | bytes 786436

commit v3 on v2

--- a/solution.py
+++ b/solution.py
@@ -39,10 +39,12 @@
 
 
 def fused_kernel(
-    inv_ref, panel_ref, mask_ref, diag_ref, off_ref, new_ref,
+    inv_ref, panel_ref, diag_ref, members_ref, counts_ref, off_ref, new_ref,
     coded, scales, wide_scale, blocks, stacked, partial, from_twin, chip_sum, from_chips,
+    late, late_partial, late_twin, late_sum, late_code, late_scale, code_in, scale_in, late_wide,
     a_recv, a_right, a_left, s_recv, s_right, s_left,
     p_recv, p_send, p_twin, t_recv, t_send, c_recv, c_send,
+    lt_recv, lt_send, lc_recv, lc_send, ls_recv, ls_send,
 ):
     n = coded.shape[0]
     rows, depth = inv_ref.shape
@@ -97,6 +99,17 @@
     def _():
         pl.semaphore_signal(barrier, inc=1, device_id=(me, z + 1), device_id_type=MESH)
 
+    sup_count = cols // B
+    masks = []
+    for k in range(sup_count):
+        sup = z * sup_count + k
+        hit = jnp.int32(0)
+        for slot in range(members_ref.shape[1]):
+            match = jnp.where(members_ref[sup, slot] == me, 1, 0)
+            hit += match * jnp.where(slot < counts_ref[sup], 1, 0)
+        masks.append(jnp.broadcast_to(hit.astype(jnp.float32), (1, B)))
+    mask = jnp.concatenate(masks, axis=1)
+
     block = inv_ref[...]
     peak = jnp.max(jnp.abs(block), axis=1, keepdims=True)
     live = peak > 1e-33
@@ -107,7 +120,7 @@
     coded[z] = ready.astype(jnp.int32).astype(jnp.int16)
     step = jnp.broadcast_to(safe * (1.0 / 32767.0), (rows, 128))
     scales[z] = step.T[:8]
-    blocks[me] = panel_ref[...] * mask_ref[...].astype(jnp.bfloat16)
+    blocks[me] = panel_ref[...] * mask.astype(jnp.bfloat16)
 
     pl.semaphore_wait(barrier, 4 + jnp.where(z > 0, 1, 0) + jnp.where(z < n - 1, 1, 0))
 
@@ -172,7 +185,7 @@
         eight = scales[c]
         wide_scale[...] = jnp.concatenate([eight] * 16, axis=0).T
 
-    def accumulate(c, first, count):
+    def accumulate(c, first, count, into, where):
         span = pl.ds(first, count)
         code = coded[c, span, :].astype(jnp.int32)
         high = (code + 64) & -128
@@ -186,7 +199,7 @@
             tile = pl.ds(pl.multiple_of(t * TILE, TILE), TILE)
             part = blocks[pl.ds(2 * c, 2), :, tile].reshape(depth, TILE)
             term = jnp.dot(stacked[0 : 2 * count], part, preferred_element_type=jnp.float32)
-            off_ref[span, tile] += step * (term[:count] + term[count:])
+            into[where, tile] += step * (term[:count] + term[count:])
 
     relay(1)
     for d in range(2):
@@ -204,53 +217,25 @@
         @pl.when((c <= z + 2) & (c >= z - 2))
         def _():
             widen(c)
-            accumulate(c, 0, rows)
-
-    end = (z == 0) | (z == n - 1)
-    last = n - 1 - z
-
-    @pl.when(z == n - 1)
-    def _():
-        right_scale(last).wait_recv()
-
-    @pl.when(z == 0)
-    def _():
-        left_scale(last).wait_recv()
-
-    @pl.when(end)
-    def _():
-        widen(last)
-
-    @pl.loop(0, pieces)
-    def _(p):
-        first = pl.multiple_of(p * PIECE, PIECE)
-        span = pl.ds(first, PIECE)
-
-        @pl.when(z == n - 1)
-        def _():
-            right_piece(last, p).wait_recv()
-
-        @pl.when(z == 0)
-        def _():
-            left_piece(last, p).wait_recv()
-
-        @pl.when(end)
-        def _():
-            accumulate(last, first, PIECE)
-
-        off = -(off_ref[span, :] * mask_ref[...])
-        off_ref[span, :] = off
-        high = off.astype(jnp.bfloat16)
-        low = (off - high.astype(jnp.float32)).astype(jnp.bfloat16)
+            accumulate(c, 0, rows, off_ref, pl.ds(0, rows))
+
+    def diag_term(value, span, into):
+        high = value.astype(jnp.bfloat16)
+        low = (value - high.astype(jnp.float32)).astype(jnp.bfloat16)
         own = blocks[me, span, :]
-        for k in range(cols // B):
+        for k in range(sup_count):
             part = slice(k * B, (k + 1) * B)
             left = jnp.concatenate([own[:, part]] * 2, axis=0)
             both = jnp.concatenate([high[:, part], low[:, part]], axis=0)
             term = lax.dot_general(
                 left, both, (((0,), (0,)), ((), ())), preferred_element_type=jnp.float32
             )
-            partial[:, :, part] += term.reshape(8, B // 8, B)
+            into[:, :, part] += term.reshape(8, B // 8, B)
+
+    @pl.loop(0, pieces)
+    def _(p):
+        span = pl.ds(pl.multiple_of(p * PIECE, PIECE), PIECE)
+        diag_term(off_ref[span, :], span, partial)
 
     def to_twin(c):
         return far(partial.at[2 * c + (1 - core)], from_twin.at[c], t_send.at[c], t_recv.at[c], twin, z)
@@ -261,20 +246,113 @@
             others[d] * 2 + core, z,
         )
 
+    def late_to_twin(c):
+        return far(
+            late_partial.at[2 * c + (1 - core)], late_twin.at[c], lt_send.at[c], lt_recv.at[c], twin, z
+        )
+
+    def late_to_chip(d):
+        return far(
+            late_code.at[others[d]], code_in.at[d], lc_send.at[d], lc_recv.at[d],
+            others[d] * 2 + core, z,
+        )
+
+    def late_scale_to_chip(d):
+        return far(late_scale, scale_in.at[d], ls_send.at[d], ls_recv.at[d], others[d] * 2 + core, z)
+
     order = (others[2], others[0], others[1], chip)
     for c in order:
         to_twin(c).start()
+    late_partial[...] = jnp.zeros_like(late_partial)
     for d in (2, 0, 1):
         c = others[d]
         to_twin(c).wait_recv()
         chip_sum[c] = partial[2 * c + core] + from_twin[c]
         to_chip(d).start()
     to_twin(chip).wait_recv()
-    total = diag_ref[...] - (partial[me] + from_twin[chip])
-    for d in (0, 1, 2):
-        to_chip(d).wait_recv()
-        total = total - from_chips[d]
-    new_ref[...] = total
+    new_ref[...] = diag_ref[...] + (partial[me] + from_twin[chip])
+
+    end = (z == 0) | (z == n - 1)
+    last = n - 1 - z
+
+    @pl.when(z == n - 1)
+    def _():
+        right_scale(last).wait_recv()
+
+    @pl.when(z == 0)
+    def _():
+        left_scale(last).wait_recv()
+
+    @pl.when(end)
+    def _():
+        widen(last)
+
+    @pl.loop(0, pieces)
+    def _(p):
+        first = pl.multiple_of(p * PIECE, PIECE)
+        span = pl.ds(first, PIECE)
+
+        @pl.when(z == n - 1)
+        def _():
+            right_piece(last, p).wait_recv()
+
+        @pl.when(z == 0)
+        def _():
+            left_piece(last, p).wait_recv()
+
+        late[...] = jnp.zeros_like(late)
+
+        @pl.when(end)
+        def _():
+            accumulate(last, first, PIECE, late, pl.ds(0, PIECE))
+            diag_term(late[...], span, late_partial)
+
+        off_ref[span, :] = -((off_ref[span, :] + late[...]) * mask)
+
+    @pl.when(end)
+    def _():
+        for c in order:
+            late_to_twin(c).start()
+        for d in range(3):
+            to_chip(d).wait_recv()
+            new_ref[...] += from_chips[d]
+        for d in (2, 0, 1):
+            c = others[d]
+            late_to_twin(c).wait_recv()
+            late_sum[c] = late_partial[2 * c + core] + late_twin[c]
+        late_to_twin(chip).wait_recv()
+        late_sum[chip] = jnp.zeros(late_sum.shape[1:], jnp.float32)
+        share = late_sum.shape[1]
+        value = late_sum[...].reshape(4 * share, cols)
+        top = jnp.max(jnp.abs(value), axis=1, keepdims=True)
+        some = top > 1e-33
+        held = jnp.where(some, top, 1.0)
+        ready = value * jnp.where(some, 32767.0 / held, 0.0)
+        ready = ready + jnp.where(ready >= 0.0, 0.5, -0.5)
+        late_code[...] = ready.astype(jnp.int32).astype(jnp.int16).reshape(4, share, cols)
+        late_scale[...] = jnp.broadcast_to(held * (1.0 / 32767.0), (4 * share, 128)).T[:8]
+        for d in (2, 0, 1):
+            late_to_chip(d).start()
+            late_scale_to_chip(d).start()
+        new_ref[...] += late_partial[me] + late_twin[chip]
+        for d in (0, 1, 2):
+            late_scale_to_chip(d).wait_recv()
+            late_to_chip(d).wait_recv()
+            late_wide[...] = jnp.concatenate([scale_in[d]] * 16, axis=0).T
+            unit = late_wide[pl.ds(pl.multiple_of(chip * share, share), share), :]
+            unit = jnp.concatenate([unit] * (cols // 128), axis=1)
+            new_ref[...] += code_in[d].astype(jnp.int32).astype(jnp.float32) * unit
+        for c in order:
+            late_to_twin(c).wait_send()
+        for d in range(3):
+            late_to_chip(d).wait_send()
+            late_scale_to_chip(d).wait_send()
+
+    @pl.when(jnp.logical_not(end))
+    def _():
+        for d in range(3):
+            to_chip(d).wait_recv()
+            new_ref[...] += from_chips[d]
 
     for c in order:
         to_twin(c).wait_send()
@@ -304,10 +382,8 @@
 def fused_body(inverse_blocks, panel, diag_inverse, members, counts):
     rows_dev, cols_dev = panel.shape
     depth = inverse_blocks.shape[1]
-    sup_count = cols_dev // B
     shards = lax.axis_size("col")
     pieces = rows_dev // PIECE
-    mask = column_masks(members, counts, lax.axis_index("row"), lax.axis_index("col") * sup_count, sup_count)
     share = diag_inverse.shape[0]
     vmem = pl.BlockSpec(memory_space=pltpu.VMEM)
     dma = pltpu.SemaphoreType.DMA
@@ -317,7 +393,7 @@
             jax.ShapeDtypeStruct((rows_dev, cols_dev), jnp.float32),
             jax.ShapeDtypeStruct((share, cols_dev), jnp.float32),
         ),
-        in_specs=[vmem] * 4,
+        in_specs=[vmem] * 3 + [pl.BlockSpec(memory_space=pltpu.SMEM)] * 2,
         out_specs=(vmem, vmem),
         scratch_shapes=[
             pltpu.VMEM((shards, rows_dev, depth), jnp.int16),
@@ -329,14 +405,24 @@
             pltpu.VMEM((4, share, cols_dev), jnp.float32),
             pltpu.VMEM((4, share, cols_dev), jnp.float32),
             pltpu.VMEM((3, share, cols_dev), jnp.float32),
+            pltpu.VMEM((PIECE, cols_dev), jnp.float32),
+            pltpu.VMEM((8, share, cols_dev), jnp.float32),
+            pltpu.VMEM((4, share, cols_dev), jnp.float32),
+            pltpu.VMEM((4, share, cols_dev), jnp.float32),
+            pltpu.VMEM((4, share, cols_dev), jnp.int16),
+            pltpu.VMEM((8, 4 * share), jnp.float32),
+            pltpu.VMEM((3, share, cols_dev), jnp.int16),
+            pltpu.VMEM((3, 8, 4 * share), jnp.float32),
+            pltpu.VMEM((4 * share, 128), jnp.float32),
             dma((shards, pieces)), dma((shards, pieces)), dma((shards, pieces)),
             dma((shards,)), dma((shards,)), dma((shards,)),
             dma((8,)), dma((3,)), dma((4,)), dma((4,)), dma((4,)), dma((3,)), dma((3,)),
+            dma((4,)), dma((4,)), dma((3,)), dma((3,)), dma((3,)), dma((3,)),
         ],
         compiler_params=pltpu.CompilerParams(
             collective_id=0, has_side_effects=True, vmem_limit_bytes=56 * 1024 * 1024
         ),
-    )(inverse_blocks, panel, mask[None, :], diag_inverse)
+    )(inverse_blocks, panel, diag_inverse, members, counts)
 
 
 def body(inverse_blocks, panel, diag_inverse, members, counts):

time: 101 us -> 100 us (0.990)
  local copies, waits for them, and re-layouts: 5.31 us -> 3.91 us
    unnamed x6 -> x4, local copies, waits for them, and re-layouts: 4.58 us -> 3.91 us
where the time goes in v3:
time: 100 us; the launch traced here: 99.9 us
  Pallas kernels  95.3 us (95%)
  local copies, waits for them, and re-layouts  3.91 us (4%)
    pallas_call x1, Pallas kernels, fused_body(): pl.pallas_call(fused_kernel, out_shape=(jax.ShapeDtypeStruct((rows_dev, c...  95.3 us
    unnamed x4, local copies, waits for them, and re-layouts  3.91 us

profile of v3, /device:TPU:0, one launch (start us, length us, event | category | flops | bytes accessed | tf_op | source)
XLA Modules:
  0.0 99.9 jit_solution(8855486214896362136)
XLA Ops:
  0.6 95.3 %shard_map.68 = (f32[512,1024]{1,0:T(8,128)}, f32[64,1024]{1,0:T(8,128)}) custom-call(f32[512,1024]{1,0:T(8,128)} %inv_ref.1, bf16[512,1024]{1,0:T(8,128)(2,1)} %panel_ref.1, f32[64,1024]{1,0:T(8,128)} %diag_ref.1, s32[8,8]{1,0:T(8,128)} %members_ref.1, s32[8]{0:T(128)} %counts_ref.1), custom_call_target="tpu_custom_call" | custom-call | tf_op jit(solution)/shard_map/pallas_call | solution.py:390
  96.0 0.0 copy-start
  96.0 3.2 %copy.9 = f32[512,1024]{1,0:T(8,128)} copy(f32[512,1024]{1,0:T(8,128)} %get-tuple-element.4) | data formatting | bytes 4194304
  99.2 0.0 copy-done
  99.2 0.7 copy.10
Async XLA Ops:
  96.0 3.2 %copy-start = (f32[64,1024]{1,0:T(8,128)S(1)}, f32[64,1024]{1,0:T(8,128)}, u32[]{:S(2)}) copy-start(f32[64,1024]{1,0:T(8,128)} %get-tuple-element.5) | copy-start | bytes 786436

commit v4 on v3

--- a/solution.py
+++ b/solution.py
@@ -43,7 +43,7 @@
     coded, scales, wide_scale, blocks, stacked, partial, from_twin, chip_sum, from_chips,
     late, late_partial, late_twin, late_sum, late_code, late_scale, code_in, scale_in, late_wide,
     a_recv, a_right, a_left, s_recv, s_right, s_left,
-    p_recv, p_send, p_twin, t_recv, t_send, c_recv, c_send,
+    p_recv, p_send, p_pass, p_twin, t_recv, t_send, c_recv, c_send,
     lt_recv, lt_send, lc_recv, lc_send, ls_recv, ls_send,
 ):
     n = coded.shape[0]
@@ -77,15 +77,23 @@
     def left_scale(c):
         return far(scales.at[c], scales.at[c], s_left.at[c], s_recv.at[c], me, z - 1)
 
-    def panel_to(d):
-        return far(blocks.at[me], blocks.at[me], p_send.at[d], p_recv.at[me], others[d] * 2 + core, z)
-
-    def panel_twin(d):
+    def half_of(r, h):
+        return blocks.at[r, pl.ds(h * (rows // 2), rows // 2)]
+
+    def panel_to(d, h):
+        ref = half_of(me, h)
+        return far(ref, ref, p_send.at[d, h], p_recv.at[me, h], others[d] * 2 + core, z)
+
+    def panel_pass(d):
+        r = others[1 - d] * 2 + core
+        return far(half_of(r, d), half_of(r, d), p_pass.at[d], p_recv.at[r, d], others[d] * 2 + core, z)
+
+    def panel_twin(d, h):
         r = me if d == 3 else others[d] * 2 + core
-        return far(blocks.at[r], blocks.at[r], p_twin.at[d], p_recv.at[r], twin, z)
-
-    def panel_arrived(r):
-        far(blocks.at[r], blocks.at[r], p_twin.at[0], p_recv.at[r], twin, z).wait_recv()
+        return far(half_of(r, h), half_of(r, h), p_twin.at[d, h], p_recv.at[r, h], twin, z)
+
+    def panel_arrived(r, h):
+        far(half_of(r, h), half_of(r, h), p_twin.at[0, 0], p_recv.at[r, h], twin, z).wait_recv()
 
     barrier = pltpu.get_barrier_semaphore()
     for row in [twin] + [o * 2 + core for o in others]:
@@ -140,9 +148,10 @@
         def _(p):
             left_piece(z, p).start()
 
-    panel_twin(3).start()
-    for d in range(3):
-        panel_to(d).start()
+    for d, h in ((0, 1), (1, 0), (0, 0), (1, 1)):
+        panel_to(d, h).start()
+    for h in range(2):
+        panel_twin(3, h).start()
     off_ref[...] = jnp.zeros_like(off_ref)
     partial[...] = jnp.zeros_like(partial)
 
@@ -201,23 +210,40 @@
             term = jnp.dot(stacked[0 : 2 * count], part, preferred_element_type=jnp.float32)
             into[where, tile] += step * (term[:count] + term[count:])
 
+    def accumulate_near(low, high):
+        @pl.loop(0, n)
+        def _(c):
+            gap = jnp.where(c > z, c - z, z - c)
+
+            @pl.when((gap >= low) & (gap <= high))
+            def _():
+                widen(c)
+                accumulate(c, 0, rows, off_ref, pl.ds(0, rows))
+
+    end = (z == 0) | (z == n - 1)
+    last = n - 1 - z
     relay(1)
     for d in range(2):
-        panel_arrived(others[d] * 2 + core)
-        panel_twin(d).start()
+        panel_arrived(others[1 - d] * 2 + core, d)
+        panel_pass(d).start()
+        panel_twin(1 - d, d).start()
+    for d in range(2):
+        panel_arrived(others[d] * 2 + core, d)
+        panel_twin(d, d).start()
+    for h in range(2):
+        panel_arrived(others[2] * 2 + core, h)
+        panel_twin(2, h).start()
+    for h in range(2):
+        panel_arrived(twin, h)
+        for d in range(3):
+            panel_arrived(others[d] * 2 + (1 - core), h)
+
+    @pl.when(end)
+    def _():
+        accumulate_near(0, 1)
+
     relay(2)
-    panel_arrived(others[2] * 2 + core)
-    panel_twin(2).start()
-    panel_arrived(twin)
-    for d in range(3):
-        panel_arrived(others[d] * 2 + (1 - core))
-
-    @pl.loop(0, n)
-    def _(c):
-        @pl.when((c <= z + 2) & (c >= z - 2))
-        def _():
-            widen(c)
-            accumulate(c, 0, rows, off_ref, pl.ds(0, rows))
+    accumulate_near(jnp.where(end, 2, 0), 2)
 
     def diag_term(value, span, into):
         high = value.astype(jnp.bfloat16)
@@ -271,9 +297,6 @@
         to_chip(d).start()
     to_twin(chip).wait_recv()
     new_ref[...] = diag_ref[...] + (partial[me] + from_twin[chip])
-
-    end = (z == 0) | (z == n - 1)
-    last = n - 1 - z
 
     @pl.when(z == n - 1)
     def _():
@@ -358,9 +381,12 @@
         to_twin(c).wait_send()
     for d in range(3):
         to_chip(d).wait_send()
-        panel_to(d).wait_send()
-    for d in range(4):
-        panel_twin(d).wait_send()
+    for h in range(2):
+        panel_pass(h).wait_send()
+        for d in range(2):
+            panel_to(d, h).wait_send()
+        for d in range(4):
+            panel_twin(d, h).wait_send()
     for s in range(3):
         @pl.when((z >= s) & (z < n - 1))
         def _():
@@ -416,7 +442,7 @@
             pltpu.VMEM((4 * share, 128), jnp.float32),
             dma((shards, pieces)), dma((shards, pieces)), dma((shards, pieces)),
             dma((shards,)), dma((shards,)), dma((shards,)),
-            dma((8,)), dma((3,)), dma((4,)), dma((4,)), dma((4,)), dma((3,)), dma((3,)),
+            dma((8, 2)), dma((2, 2)), dma((2,)), dma((4, 2)), dma((4,)), dma((4,)), dma((3,)), dma((3,)),
             dma((4,)), dma((4,)), dma((3,)), dma((3,)), dma((3,)), dma((3,)),
         ],
         compiler_params=pltpu.CompilerParams(

time: 100 us -> 95.1 us (0.951)
  Pallas kernels: 95.3 us -> 90.2 us
    pallas_call x1, Pallas kernels: 95.3 us -> 90.2 us  [fused_body(): pl.pallas_call(fused_kernel, out_shape=(jax.ShapeDtypeStruct((rows_dev, c...]
where the time goes in v4:
time: 95.1 us; the launch traced here: 94.8 us
  Pallas kernels  90.2 us (95%)
  local copies, waits for them, and re-layouts  3.91 us (4%)
    pallas_call x1, Pallas kernels, fused_body(): pl.pallas_call(fused_kernel, out_shape=(jax.ShapeDtypeStruct((rows_dev, c...  90.2 us
    unnamed x4, local copies, waits for them, and re-layouts  3.91 us

profile of v4, /device:TPU:0, one launch (start us, length us, event | category | flops | bytes accessed | tf_op | source)
XLA Modules:
  0.0 94.8 jit_solution(17324408398699993037)
XLA Ops:
  0.6 90.2 %shard_map.68 = (f32[512,1024]{1,0:T(8,128)}, f32[64,1024]{1,0:T(8,128)}) custom-call(f32[512,1024]{1,0:T(8,128)} %inv_ref.1, bf16[512,1024]{1,0:T(8,128)(2,1)} %panel_ref.1, f32[64,1024]{1,0:T(8,128)} %diag_ref.1, s32[8,8]{1,0:T(8,128)} %members_ref.1, s32[8]{0:T(128)} %counts_ref.1), custom_call_target="tpu_custom_call" | custom-call | tf_op jit(solution)/shard_map/pallas_call | solution.py:416
  90.8 0.0 copy-start
  90.8 3.2 %copy.9 = f32[512,1024]{1,0:T(8,128)} copy(f32[512,1024]{1,0:T(8,128)} %get-tuple-element.4) | data formatting | bytes 4194304
  94.0 0.0 copy-done
  94.0 0.7 copy.10
Async XLA Ops:
  90.8 3.2 %copy-start = (f32[64,1024]{1,0:T(8,128)S(1)}, f32[64,1024]{1,0:T(8,128)}, u32[]{:S(2)}) copy-start(f32[64,1024]{1,0:T(8,128)} %get-tuple-element.5) | copy-start | bytes 786436

commit v5 on v4

--- a/solution.py
+++ b/solution.py
@@ -39,7 +39,8 @@
 
 
 def fused_kernel(
-    inv_ref, panel_ref, diag_ref, members_ref, counts_ref, off_ref, new_ref,
+    inv_hbm, panel_hbm, diag_hbm, members_hbm, counts_hbm, off_ref, new_ref,
+    inv_ref, panel_ref, diag_ref, members_ref, counts_ref, load,
     coded, scales, wide_scale, blocks, stacked, partial, from_twin, chip_sum, from_chips,
     late, late_partial, late_twin, late_sum, late_code, late_scale, code_in, scale_in, late_wide,
     a_recv, a_right, a_left, s_recv, s_right, s_left,
@@ -47,8 +48,8 @@
     lt_recv, lt_send, lc_recv, lc_send, ls_recv, ls_send,
 ):
     n = coded.shape[0]
-    rows, depth = inv_ref.shape
-    cols = panel_ref.shape[1]
+    rows, depth = inv_hbm.shape
+    cols = panel_hbm.shape[1]
     pieces = rows // PIECE
     me = lax.axis_index("row")
     z = lax.axis_index("col")
@@ -63,12 +64,17 @@
             device_id=(row, col), device_id_type=MESH,
         )
 
+    def rows_of(p):
+        if isinstance(p, int):
+            return pl.ds(p * PIECE, PIECE)
+        return pl.ds(pl.multiple_of(p * PIECE, PIECE), PIECE)
+
     def right_piece(c, p):
-        ref = coded.at[c, pl.ds(pl.multiple_of(p * PIECE, PIECE), PIECE)]
+        ref = coded.at[c, rows_of(p)]
         return far(ref, ref, a_right.at[c, p], a_recv.at[c, p], me, z + 1)
 
     def left_piece(c, p):
-        ref = coded.at[c, pl.ds(pl.multiple_of(p * PIECE, PIECE), PIECE)]
+        ref = coded.at[c, rows_of(p)]
         return far(ref, ref, a_left.at[c, p], a_recv.at[c, p], me, z - 1)
 
     def right_scale(c):
@@ -95,6 +101,17 @@
     def panel_arrived(r, h):
         far(half_of(r, h), half_of(r, h), p_twin.at[0, 0], p_recv.at[r, h], twin, z).wait_recv()
 
+    loads = [
+        pltpu.make_async_copy(src, dst, load.at[i])
+        for i, (src, dst) in enumerate(
+            (
+                (inv_hbm, inv_ref), (members_hbm, members_ref), (counts_hbm, counts_ref),
+                (panel_hbm, panel_ref), (diag_hbm, diag_ref),
+            )
+        )
+    ]
+    for copy in loads:
+        copy.start()
     barrier = pltpu.get_barrier_semaphore()
     for row in [twin] + [o * 2 + core for o in others]:
         pl.semaphore_signal(barrier, inc=1, device_id=(row, z), device_id_type=MESH)
@@ -107,6 +124,39 @@
     def _():
         pl.semaphore_signal(barrier, inc=1, device_id=(me, z + 1), device_id_type=MESH)
 
+    loads[0].wait()
+    peak = jnp.max(jnp.abs(inv_ref[...]), axis=1, keepdims=True)
+    live = peak > 1e-33
+    safe = jnp.where(live, peak, 1.0)
+    ratio = jnp.where(live, 32767.0 / safe, 0.0)
+    step = jnp.broadcast_to(safe * (1.0 / 32767.0), (rows, 128))
+    scales[z] = step.T[:8]
+    pl.semaphore_wait(barrier, 4 + jnp.where(z > 0, 1, 0) + jnp.where(z < n - 1, 1, 0))
+
+    @pl.when(z < n - 1)
+    def _():
+        right_scale(z).start()
+
+    @pl.when(z > 0)
+    def _():
+        left_scale(z).start()
+
+    for p in range(pieces):
+        span = slice(p * PIECE, (p + 1) * PIECE)
+        ready = inv_ref[span, :] * ratio[span]
+        ready = ready + jnp.where(ready >= 0.0, 0.5, -0.5)
+        coded[z, span, :] = ready.astype(jnp.int32).astype(jnp.int16)
+
+        @pl.when(z < n - 1)
+        def _():
+            right_piece(z, p).start()
+
+        @pl.when(z > 0)
+        def _():
+            left_piece(z, p).start()
+
+    for copy in loads[1:]:
+        copy.wait()
     sup_count = cols // B
     masks = []
     for k in range(sup_count):
@@ -118,36 +168,7 @@
         masks.append(jnp.broadcast_to(hit.astype(jnp.float32), (1, B)))
     mask = jnp.concatenate(masks, axis=1)
 
-    block = inv_ref[...]
-    peak = jnp.max(jnp.abs(block), axis=1, keepdims=True)
-    live = peak > 1e-33
-    safe = jnp.where(live, peak, 1.0)
-    ratio = jnp.where(live, 32767.0 / safe, 0.0)
-    ready = block * ratio
-    ready = ready + jnp.where(ready >= 0.0, 0.5, -0.5)
-    coded[z] = ready.astype(jnp.int32).astype(jnp.int16)
-    step = jnp.broadcast_to(safe * (1.0 / 32767.0), (rows, 128))
-    scales[z] = step.T[:8]
     blocks[me] = panel_ref[...] * mask.astype(jnp.bfloat16)
-
-    pl.semaphore_wait(barrier, 4 + jnp.where(z > 0, 1, 0) + jnp.where(z < n - 1, 1, 0))
-
-    @pl.when(z < n - 1)
-    def _():
-        right_scale(z).start()
-
-        @pl.loop(0, pieces)
-        def _(p):
-            right_piece(z, p).start()
-
-    @pl.when(z > 0)
-    def _():
-        left_scale(z).start()
-
-        @pl.loop(0, pieces)
-        def _(p):
-            left_piece(z, p).start()
-
     for d, h in ((0, 1), (1, 0), (0, 0), (1, 1)):
         panel_to(d, h).start()
     for h in range(2):
@@ -419,9 +440,15 @@
             jax.ShapeDtypeStruct((rows_dev, cols_dev), jnp.float32),
             jax.ShapeDtypeStruct((share, cols_dev), jnp.float32),
         ),
-        in_specs=[vmem] * 3 + [pl.BlockSpec(memory_space=pltpu.SMEM)] * 2,
+        in_specs=[pl.BlockSpec(memory_space=pltpu.HBM)] * 5,
         out_specs=(vmem, vmem),
         scratch_shapes=[
+            pltpu.VMEM(inverse_blocks.shape, jnp.float32),
+            pltpu.VMEM(panel.shape, jnp.bfloat16),
+            pltpu.VMEM(diag_inverse.shape, jnp.float32),
+            pltpu.SMEM(members.shape, jnp.int32),
+            pltpu.SMEM(counts.shape, jnp.int32),
+            dma((5,)),
             pltpu.VMEM((shards, rows_dev, depth), jnp.int16),
             pltpu.VMEM((shards, 8, rows_dev), jnp.float32),
             pltpu.VMEM((rows_dev, 128), jnp.float32),

time: 95.1 us -> 94.1 us (0.989)
  no operation moved by 1% of the time
where the time goes in v5:
time: 94.1 us; the launch traced here: 94 us
  Pallas kernels  89.4 us (95%)
  local copies, waits for them, and re-layouts  3.91 us (4%)
    pallas_call x1, Pallas kernels, fused_body(): pl.pallas_call(fused_kernel, out_shape=(jax.ShapeDtypeStruct((rows_dev, c...  89.4 us
    unnamed x4, local copies, waits for them, and re-layouts  3.91 us

profile of v5, /device:TPU:0, one launch (start us, length us, event | category | flops | bytes accessed | tf_op | source)
XLA Modules:
  0.0 94.0 jit_solution(16926509989066434861)
XLA Ops:
  0.6 89.4 %shard_map.68 = (f32[512,1024]{1,0:T(8,128)}, f32[64,1024]{1,0:T(8,128)}) custom-call(f32[512,1024]{1,0:T(8,128)} %inv_hbm.1, bf16[512,1024]{1,0:T(8,128)(2,1)} %panel_hbm.1, f32[64,1024]{1,0:T(8,128)} %diag_hbm.1, s32[8,8]{1,0:T(8,128)} %members_hbm.1, s32[8]{0:T(128)} %counts_hbm.1), custom_call_target="tpu_custom_call" | custom-call | tf_op jit(solution)/shard_map/pallas_call | solution.py:437
  90.1 0.0 copy-start
  90.1 3.2 %copy.9 = f32[512,1024]{1,0:T(8,128)} copy(f32[512,1024]{1,0:T(8,128)} %get-tuple-element.4) | data formatting | bytes 4194304
  93.3 0.0 copy-done
  93.3 0.7 copy.10
Async XLA Ops:
  90.1 3.2 %copy-start = (f32[64,1024]{1,0:T(8,128)S(1)}, f32[64,1024]{1,0:T(8,128)}, u32[]{:S(2)}) copy-start(f32[64,1024]{1,0:T(8,128)} %get-tuple-element.5) | copy-start | bytes 786436
